TPU v7x, 128 devices: a whole 4x4x4 slice. The times are simulated.
128 devices in a mesh: row: 16 (over y, x), col: 8 (over z, core).
Axes of the slice: x: 4, y: 4, z: 4, core: 2. Of those that a mesh axis runs over, the one named last changes fastest.
Arguments:
- layer_input: bfloat16 [768, 8192], P('col', 'row'), may hold values from -6 to 6
- out_grad: bfloat16 [768, 8192], P('col', 'row'), may hold values from -6 to 6
- gate_weight: bfloat16 [8192, 28672], P('row', 'col'), may hold values from -0.0625 to 0.0625
- up_weight: bfloat16 [8192, 28672], P('row', 'col'), may hold values from -0.0625 to 0.0625
- down_weight: bfloat16 [28672, 8192], P('col', 'row'), may hold values from -0.03125 to 0.03125
Outputs:
- input_grad: bfloat16 [768, 8192], P('col', 'row')
- gate_grad: bfloat16 [8192, 28672], P('row', 'col')
- up_grad: bfloat16 [8192, 28672], P('row', 'col')
- down_grad: bfloat16 [28672, 8192], P('col', 'row')
All inputs are finite; a program needn't handle non-finite values.
Results may differ from a plain program's by a relative error of at most 0.033.
Values may be sent and summed in bfloat16 or wider, within the bound.
A program may use at most 192 MiB of HBM per device.

v0:
```python
import jax
import jax.numpy as jnp
from jax import lax
from jax.sharding import PartitionSpec as P


def swiglu_back(summed, width):
    gate = summed[:, :width]
    up = summed[:, width : 2 * width]
    hidden_grad = summed[:, 2 * width :]
    sigma = jax.nn.sigmoid(gate)
    swish = gate * sigma
    hidden = (swish * up).astype(jnp.bfloat16)
    up_delta = (hidden_grad * swish).astype(jnp.bfloat16)
    gate_delta = (hidden_grad * up * sigma * (1.0 + gate * (1.0 - sigma))).astype(jnp.bfloat16)
    return (hidden, gate_delta, up_delta)


def local(layer_input, out_grad, gate_weight, up_weight, down_weight):
    input_rows, cot_rows = (
        lax.all_gather(layer_input, "col", axis=0, tiled=True),
        lax.all_gather(out_grad, "col", axis=0, tiled=True),
    )
    tokens = input_rows.shape[0]
    width = gate_weight.shape[1]
    both_weights = jnp.concatenate([gate_weight, up_weight], axis=1)
    contract_last = (((1,), (1,)), ((), ()))
    contract_first = (((0,), (0,)), ((), ()))
    left = input_rows
    right = cot_rows
    gate_up = jnp.dot(left, both_weights, preferred_element_type=jnp.float32)
    hidden_grad = lax.dot_general(
        right, down_weight, contract_last, preferred_element_type=jnp.float32
    )
    summed = lax.psum_scatter(
        jnp.concatenate([gate_up, hidden_grad], axis=1).astype(jnp.bfloat16),
        "row",
        scatter_dimension=0,
        tiled=True,
    ).astype(jnp.float32)
    hidden, gate_delta, up_delta = swiglu_back(summed, width)
    accumulate_hidden = lax.all_gather(hidden, "row", axis=0, tiled=True)
    accumulate_gate_delta = lax.all_gather(gate_delta, "row", axis=0, tiled=True)
    accumulate_up_delta = lax.all_gather(up_delta, "row", axis=0, tiled=True)
    left = input_rows
    right = cot_rows
    down_sum = lax.dot_general(
        accumulate_hidden, right, contract_first, preferred_element_type=jnp.float32
    )
    gate_sum = lax.dot_general(
        left, accumulate_gate_delta, contract_first, preferred_element_type=jnp.float32
    )
    up_sum = lax.dot_general(
        left, accumulate_up_delta, contract_first, preferred_element_type=jnp.float32
    )
    term = lax.dot_general(
        accumulate_gate_delta, gate_weight, contract_last, preferred_element_type=jnp.float32
    )
    term = term + lax.dot_general(
        accumulate_up_delta, up_weight, contract_last, preferred_element_type=jnp.float32
    )
    factor = 1.0 / tokens**0.5
    down_grad = (down_sum * factor).astype(jnp.bfloat16)
    gate_grad = (gate_sum * factor).astype(jnp.bfloat16)
    up_grad = (up_sum * factor).astype(jnp.bfloat16)
    input_grad = lax.psum_scatter(term.astype(jnp.bfloat16), "col", scatter_dimension=0, tiled=True)
    return (input_grad, gate_grad, up_grad, down_grad)


def solution(mesh):
    placed = (P("col", "row"), P("col", "row"), P("row", "col"), P("row", "col"), P("col", "row"))
    return jax.shard_map(
        local,
        mesh=mesh,
        in_specs=placed,
        out_specs=(P("col", "row"), P("row", "col"), P("row", "col"), P("col", "row")),
        check_vma=False,
    )
```

profile of v0, /device:TPU:0, one launch (start us, length us, event | category | flops | bytes accessed | tf_op | source)
XLA Modules:
  0.0 429.2 jit_solution(3540597175312089114)
XLA Ops:
  7.2 14.9 %all_gather.15 = bf16[768,512]{1,0:T(8,128)(2,1)S(1)} all-gather(bf16[96,512]{1,0:T(8,128)(2,1)} %param.5), channel_id=1, replica_groups=mesh['row'=16,'col'=8] {'col'}, dimensions={0}, use_global_device_ids=true | all-gather | bytes 884736 | tf_op jit(solution)/shard_map/all_gather | solution.py:21
  22.1 13.6 %all_gather.16 = bf16[768,512]{1,0:T(8,128)(2,1)S(1)} all-gather(bf16[96,512]{1,0:T(8,128)(2,1)} %param.6), channel_id=1, replica_groups=mesh['row'=16,'col'=8] {'col'}, dimensions={0}, use_global_device_ids=true | all-gather | bytes 884736 | tf_op jit(solution)/shard_map/all_gather | solution.py:22
  35.7 7.5 %convolution_convert_fusion.1 = bf16[768,3584]{0,1:T(8,128)(2,1)} fusion(bf16[768,512]{1,0:T(8,128)(2,1)S(1)} %all_gather.16, bf16[3584,512]{1,0:T(8,128)(2,1)} %param.9), kind=kOutput, calls=%fused_computation.9 | convolution fusion | flops 2821324800 | bytes 9961472 | tf_op jit(solution)/shard_map/dot_general | solution.py:32
  43.2 13.8 %fusion = bf16[768,7168]{0,1:T(8,128)(2,1)} fusion(bf16[768,512]{1,0:T(8,128)(2,1)S(1)} %all_gather.15, bf16[512,3584]{1,0:T(8,128)(2,1)} %param.8, bf16[512,3584]{1,0:T(8,128)(2,1)} %param.7), kind=kOutput, calls=%fused_computation.2 | convolution fusion | flops 5657329664 | bytes 19136512 | tf_op jit(solution)/shard_map/dot_general | solution.py:31
  57.0 18.5 %pad_maximum_fusion = bf16[768,10752]{0,1:T(8,128)(2,1)} fusion(bf16[768,3584]{0,1:T(8,128)(2,1)} %convolution_convert_fusion.1, bf16[768,7168]{0,1:T(8,128)(2,1)} %fusion), kind=kLoop, calls=%fused_computation | loop fusion | flops 33030144 | bytes 33030144 | tf_op jit(solution)/shard_map/concatenate | solution.py:36
  75.5 22.3 %copy.23 = bf16[768,10752]{1,0:T(8,128)(2,1)} copy(bf16[768,10752]{0,1:T(8,128)(2,1)} %pad_maximum_fusion) | data formatting | bytes 33030144
  97.8 0.0 all-gather.4.cloned.1.call-start
  97.9 110.7 %reduce-scatter.7.cloned.1.call-done = bf16[48,10752]{1,0:T(8,128)(2,1)} async-done(((bf16[768,10752]{1,0:T(8,128)(2,1)}), bf16[48,10752]{1,0:T(8,128)(2,1)}) %reduce-scatter.7.cloned.1.call-update) | async-done | bytes 1032208 | tf_op jit(solution)/shard_map/reduce_scatter | solution.py:35
  208.6 1.4 convert_element_type.31
  210.0 1.3 multiply_convert_fusion.3
  211.3 0.7 all-gather.6.cloned.1.call-update
  212.1 0.5 all-gather.8.cloned.1.call-update
  212.6 0.2 reduce-scatter.5.cloned.1.call-start
  212.8 55.8 %all-gather.4.cloned.1.call-done = bf16[768,3584]{1,0:T(8,128)(2,1)} async-done(((bf16[48,3584]{1,0:T(8,128)(2,1)}), bf16[768,3584]{1,0:T(8,128)(2,1)}) %all-gather.4.cloned.1.call-update) | async-done | bytes 5505040 | tf_op jit(solution)/shard_map/all_gather | solution.py:43
  268.6 6.1 %fusion.8 = f32[768,512]{1,0:T(8,128)S(1)} fusion(bf16[768,3584]{1,0:T(8,128)(2,1)} %all-gather.4.cloned.1.call-done, bf16[512,3584]{1,0:T(8,128)(2,1)} %param.7), kind=kOutput, calls=%fused_computation.19 | convolution fusion | flops 2818572288 | bytes 10747904 | tf_op jit(solution)/shard_map/dot_general | solution.py:56
  274.8 54.1 %all-gather.6.cloned.1.call-done = bf16[768,3584]{1,0:T(8,128)(2,1)} async-done(((bf16[48,3584]{1,0:T(8,128)(2,1)}), bf16[768,3584]{1,0:T(8,128)(2,1)}) %all-gather.6.cloned.1.call-update) | async-done | bytes 5505040 | tf_op jit(solution)/shard_map/all_gather | solution.py:44
  328.8 7.6 %add_convert_fusion = bf16[768,512]{1,0:T(8,128)(2,1)} fusion(f32[768,512]{1,0:T(8,128)S(1)} %fusion.8, bf16[768,3584]{1,0:T(8,128)(2,1)} %all-gather.6.cloned.1.call-done, bf16[512,3584]{1,0:T(8,128)(2,1)} %param.8), kind=kOutput, calls=%fused_computation.12 | convolution fusion | flops 2819358720 | bytes 11534336 | tf_op jit(solution)/shard_map/dot_general | solution.py:59
  336.5 7.1 %fusion.5 = bf16[512,3584]{0,1:T(8,128)(2,1)} fusion(bf16[768,3584]{1,0:T(8,128)(2,1)} %all-gather.6.cloned.1.call-done, bf16[768,512]{1,0:T(8,128)(2,1)S(1)} %all_gather.15), kind=kOutput, calls=%fused_computation.11 | convolution fusion | flops 2822242304 | bytes 9961472 | tf_op jit(solution)/shard_map/dot_general | solution.py:53
  343.6 5.9 %copy.21 = bf16[512,3584]{1,0:T(8,128)(2,1)} copy(bf16[512,3584]{0,1:T(8,128)(2,1)} %fusion.5) | data formatting | bytes 7340032
  349.5 7.1 %fusion.4 = bf16[512,3584]{0,1:T(8,128)(2,1)} fusion(bf16[768,3584]{1,0:T(8,128)(2,1)} %all-gather.4.cloned.1.call-done, bf16[768,512]{1,0:T(8,128)(2,1)S(1)} %all_gather.15), kind=kOutput, calls=%fused_computation.10 | convolution fusion | flops 2822242304 | bytes 9961472 | tf_op jit(solution)/shard_map/dot_general | solution.py:50
  356.6 5.9 %copy.20 = bf16[512,3584]{1,0:T(8,128)(2,1)} copy(bf16[512,3584]{0,1:T(8,128)(2,1)} %fusion.4) | data formatting | bytes 7340032
  362.5 25.8 %all-gather.8.cloned.1.call-done = bf16[768,3584]{1,0:T(8,128)(2,1)} async-done(((bf16[48,3584]{1,0:T(8,128)(2,1)}), bf16[768,3584]{1,0:T(8,128)(2,1)}) %all-gather.8.cloned.1.call-update) | async-done | bytes 5505040 | tf_op jit(solution)/shard_map/all_gather | solution.py:42
  388.3 7.1 %multiply_convert_fusion = bf16[3584,512]{1,0:T(8,128)(2,1)} fusion(bf16[768,3584]{1,0:T(8,128)(2,1)} %all-gather.8.cloned.1.call-done, bf16[768,512]{1,0:T(8,128)(2,1)S(1)} %all_gather.16), kind=kOutput, calls=%fused_computation.6 | convolution fusion | flops 2822242304 | bytes 9961472 | tf_op jit(solution)/shard_map/dot_general | solution.py:47
  395.4 27.2 %reduce-scatter.5.cloned.1.call-done = bf16[96,512]{1,0:T(8,128)(2,1)} async-done(((bf16[768,512]{1,0:T(8,128)(2,1)}), bf16[96,512]{1,0:T(8,128)(2,1)}) %reduce-scatter.5.cloned.1.call-update) | async-done | bytes 98320 | tf_op jit(solution)/shard_map/reduce_scatter | solution.py:66
  (6 shorter events, 0.2 us)
Async XLA Ops:
  7.2 201.5 %reduce-scatter.7.cloned.1.call-start = ((), (), s32[]{:S(2)}) async-start(), calls=%async_computation.6 | async-start | bytes 17547264 | tf_op jit(solution)/shard_map/reduce_scatter | solution.py:35
  97.8 170.8 %all-gather.4.cloned.1.call-start = ((), (), s32[]{:S(2)}) async-start(), calls=%async_computation.2 | async-start | bytes 5849088 | tf_op jit(solution)/shard_map/all_gather | solution.py:43
  211.3 117.5 %all-gather.6.cloned.1.call-start = ((), (), s32[]{:S(2)}) async-start(), calls=%async_computation.3 | async-start | bytes 5849088 | tf_op jit(solution)/shard_map/all_gather | solution.py:44
  212.0 176.3 %all-gather.8.cloned.1.call-start = ((), (), s32[]{:S(2)}) async-start(), calls=%async_computation.5 | async-start | bytes 5849088 | tf_op jit(solution)/shard_map/all_gather | solution.py:42
  212.6 210.0 %reduce-scatter.5.cloned.1.call-start = ((), (), s32[]{:S(2)}) async-start(), calls=%async_computation.4 | async-start | bytes 884736 | tf_op jit(solution)/shard_map/reduce_scatter | solution.py:66
Sparse Core Ops, SparseCore 0:
  98.0 110.6 reduce-scatter.6
  211.6 57.0 all-gather.3
  271.6 57.2 all-gather.5
  331.1 57.2 all-gather.7
  391.3 31.3 reduce-scatter.4
where the time goes:
time: 430 us; the launch traced here: 429 us
  waiting for transfers between devices  275 us (64%)
  matrix products  56.3 us (13%)
  local copies, waits for them, and re-layouts  34.2 us (8%)
  blocking collectives  28.5 us (7%)
  other arithmetic  21.2 us (5%)
  between operations  13.8 us (3%)
    reduce_scatter x1, waiting for transfers between devices, local(): lax.psum_scatter(jnp.concatenate([gate_up, hidden_grad], axis=1).astype(j...  111 us
    all_gather x1, waiting for transfers between devices, local(): lax.all_gather(gate_delta, 'row', axis=0, tiled=True)  55.8 us
    all_gather x1, waiting for transfers between devices, local(): accumulate_up_delta = lax.all_gather(up_delta, 'row', axis=0, tiled=True)  54.1 us
    unnamed x3, local copies, waits for them, and re-layouts  34.2 us
    reduce_scatter x1, waiting for transfers between devices, local(): lax.psum_scatter(term.astype(jnp.bfloat16), 'col', scatter_dimension=0, t...  27.2 us
    all_gather x1, waiting for transfers between devices, local(): accumulate_hidden = lax.all_gather(hidden, 'row', axis=0, tiled=True)  25.8 us
    concatenate x1, other arithmetic, local(): jnp.concatenate([gate_up, hidden_grad], axis=1).astype(jnp.bfloat16)  18.5 us
    all_gather x1, blocking collectives, local(): lax.all_gather(layer_input, 'col', axis=0, tiled=True)  14.9 us
  transfers between devices with their start and end apart: 5, of which 5 were waited for; matrix products, arithmetic and copies ran while one was open for 11% of the time, Pallas kernels for 0%

commit v1 on v0

--- a/solution.py
+++ b/solution.py
@@ -2,6 +2,12 @@
 import jax.numpy as jnp
 from jax import lax
 from jax.sharding import PartitionSpec as P
+
+
+def in_order(pieces, dim):
+    shape = list(pieces.shape[1:])
+    shape[dim] *= pieces.shape[0]
+    return jnp.moveaxis(pieces, 0, dim).reshape(shape)
 
 
 def swiglu_back(summed, width):
@@ -39,7 +45,19 @@
         tiled=True,
     ).astype(jnp.float32)
     hidden, gate_delta, up_delta = swiglu_back(summed, width)
-    accumulate_hidden = lax.all_gather(hidden, "row", axis=0, tiled=True)
+    devices = lax.axis_size("row")
+    pairs = [(i, (i + 1) % devices) for i in range(devices)]
+    back = [(b, a) for a, b in pairs]
+    lower, upper = ([], [])
+    for step in range(devices - 1):
+        if step % 2 == 0:
+            lower.append(lax.ppermute(lower[-1] if lower else hidden, "row", pairs))
+        else:
+            upper.append(lax.ppermute(upper[-1] if upper else hidden, "row", back))
+    blocks = jnp.stack([*lower[::-1], hidden, *upper])
+    shift = lax.axis_index("row") - len(lower)
+    blocks = blocks[(jnp.arange(devices) - shift) % devices]
+    accumulate_hidden = in_order(blocks, 0)
     accumulate_gate_delta = lax.all_gather(gate_delta, "row", axis=0, tiled=True)
     accumulate_up_delta = lax.all_gather(up_delta, "row", axis=0, tiled=True)
     left = input_rows

time: 430 us -> 422 us (0.981)
  waiting for transfers between devices: 275 us -> 198 us
  starting transfers between devices: 0.38 us -> 40.7 us
  local copies, waits for them, and re-layouts: 34.2 us -> 60.9 us
    ppermute x0 -> x15, waiting for transfers between devices: none -> 71 us  [the longest x8 59.8 us: local(): lower.append(lax.ppermute(lower[-1] if lower else hidden, 'row', pairs))]
    all_gather x1, waiting for transfers between devices: 55.8 us -> 0.01 us  [local(): lax.all_gather(gate_delta, 'row', axis=0, tiled=True)]
    ppermute x0 -> x15, starting transfers between devices: none -> 40.5 us  [the longest x7 39.2 us: local(): upper.append(lax.ppermute(upper[-1] if upper else hidden, 'row', back))]
    all_gather x1, waiting for transfers between devices: 54.1 us -> 15.9 us  [local(): accumulate_up_delta = lax.all_gather(up_delta, 'row', axis=0, tiled=True)]
    reduce_scatter x1, waiting for transfers between devices: 27.2 us -> 0.01 us  [local(): lax.psum_scatter(term.astype(jnp.bfloat16), 'col', scatter_dimension=0, t...]
    all_gather x1 -> x0, waiting for transfers between devices: 25.8 us -> none  [local(): accumulate_hidden = lax.all_gather(hidden, 'row', axis=0, tiled=True)]
    unnamed x3 -> x34, local copies, waits for them, and re-layouts: 34.2 us -> 54.2 us
    gather x0 -> x1, local copies, waits for them, and re-layouts: none -> 5.95 us  [local(): blocks = blocks[(jnp.arange(devices) - shift) % devices]]
  transfers between devices with their start and end apart: 5 -> 19, of which waited for: 5 -> 12; matrix products, arithmetic and copies ran while one was open for 11% -> 16% of each run, Pallas kernels for 0% -> 0%
where the time goes in v1:
time: 422 us; the launch traced here: 419 us
  waiting for transfers between devices  198 us (47%)
  local copies, waits for them, and re-layouts  60.9 us (14%)
  matrix products  56.5 us (13%)
  starting transfers between devices  40.7 us (10%)
  blocking collectives  28.5 us (7%)
  other arithmetic  21.1 us (5%)
  between operations  13.9 us (3%)
    reduce_scatter x1, waiting for transfers between devices, local(): lax.psum_scatter(jnp.concatenate([gate_up, hidden_grad], axis=1).astype(j...  111 us
    ppermute x8, waiting for transfers between devices, local(): lower.append(lax.ppermute(lower[-1] if lower else hidden, 'row', pairs))  59.8 us
    unnamed x34, local copies, waits for them, and re-layouts  54.2 us
    ppermute x7, starting transfers between devices, local(): upper.append(lax.ppermute(upper[-1] if upper else hidden, 'row', back))  39.2 us
    concatenate x1, other arithmetic, local(): jnp.concatenate([gate_up, hidden_grad], axis=1).astype(jnp.bfloat16)  18.5 us
    all_gather x1, waiting for transfers between devices, local(): accumulate_up_delta = lax.all_gather(up_delta, 'row', axis=0, tiled=True)  15.9 us
    all_gather x1, blocking collectives, local(): lax.all_gather(layer_input, 'col', axis=0, tiled=True)  14.9 us
    dot_general x1, matrix products, local(): gate_up = jnp.dot(left, both_weights, preferred_element_type=jnp.float32)  13.8 us
  transfers between devices with their start and end apart: 19, of which 12 were waited for; matrix products, arithmetic and copies ran while one was open for 16% of the time, Pallas kernels for 0%

profile of v1, /device:TPU:0, one launch (start us, length us, event | category | flops | bytes accessed | tf_op | source)
XLA Modules:
  0.0 419.2 jit_solution(1843405410841983455)
XLA Ops:
  7.2 14.9 %all_gather.12 = bf16[768,512]{1,0:T(8,128)(2,1)S(1)} all-gather(bf16[96,512]{1,0:T(8,128)(2,1)} %param.5), channel_id=1, replica_groups=mesh['row'=16,'col'=8] {'col'}, dimensions={0}, use_global_device_ids=true | all-gather | bytes 884736 | tf_op jit(solution)/shard_map/all_gather | solution.py:27
  22.1 13.6 %all_gather.13 = bf16[768,512]{1,0:T(8,128)(2,1)S(1)} all-gather(bf16[96,512]{1,0:T(8,128)(2,1)} %param.6), channel_id=1, replica_groups=mesh['row'=16,'col'=8] {'col'}, dimensions={0}, use_global_device_ids=true | all-gather | bytes 884736 | tf_op jit(solution)/shard_map/all_gather | solution.py:28
  35.7 7.4 %convolution_convert_fusion.1 = bf16[768,3584]{0,1:T(8,128)(2,1)} fusion(bf16[768,512]{1,0:T(8,128)(2,1)S(1)} %all_gather.13, bf16[3584,512]{1,0:T(8,128)(2,1)} %param.9), kind=kOutput, calls=%fused_computation.10 | convolution fusion | flops 2821324800 | bytes 9961472 | tf_op jit(solution)/shard_map/dot_general | solution.py:38
  43.2 13.8 %fusion = bf16[768,7168]{0,1:T(8,128)(2,1)} fusion(bf16[768,512]{1,0:T(8,128)(2,1)S(1)} %all_gather.12, bf16[512,3584]{1,0:T(8,128)(2,1)} %param.8, bf16[512,3584]{1,0:T(8,128)(2,1)} %param.7), kind=kOutput, calls=%fused_computation.3 | convolution fusion | flops 5657329664 | bytes 19136512 | tf_op jit(solution)/shard_map/dot_general | solution.py:37
  57.0 18.5 %pad_maximum_fusion = bf16[768,10752]{0,1:T(8,128)(2,1)} fusion(bf16[768,3584]{0,1:T(8,128)(2,1)} %convolution_convert_fusion.1, bf16[768,7168]{0,1:T(8,128)(2,1)} %fusion), kind=kLoop, calls=%fused_computation.1 | loop fusion | flops 33030144 | bytes 33030144 | tf_op jit(solution)/shard_map/concatenate | solution.py:42
  75.4 22.3 %copy.29 = bf16[768,10752]{1,0:T(8,128)(2,1)} copy(bf16[768,10752]{0,1:T(8,128)(2,1)} %pad_maximum_fusion) | data formatting | bytes 33030144
  97.9 110.7 %reduce-scatter.7.cloned.1.call-done = bf16[48,10752]{1,0:T(8,128)(2,1)} async-done(((bf16[768,10752]{1,0:T(8,128)(2,1)}), bf16[48,10752]{1,0:T(8,128)(2,1)}) %reduce-scatter.7.cloned.1.call-update) | async-done | bytes 1032208 | tf_op jit(solution)/shard_map/reduce_scatter | solution.py:41
  212.4 11.6 %collective-permute-done = bf16[48,3584]{1,0:T(8,128)(2,1)S(1)} collective-permute-done((bf16[48,3584]{1,0:T(8,128)(2,1)S(1)}, bf16[48,3584]{1,0:T(8,128)(2,1)S(1)}, u32[]{:S(2)}, u32[]{:S(2)}) %collective-permute-start) | collective-permute-done | bytes 344096 | tf_op jit(solution)/shard_map/ppermute | solution.py:54
  229.4 10.7 %collective-permute-done.1 = bf16[48,3584]{1,0:T(8,128)(2,1)S(1)} collective-permute-done((bf16[48,3584]{1,0:T(8,128)(2,1)S(1)}, bf16[48,3584]{1,0:T(8,128)(2,1)S(1)}, u32[]{:S(2)}, u32[]{:S(2)}) %collective-permute-start.1) | collective-permute-done | bytes 344096 | tf_op jit(solution)/shard_map/ppermute | solution.py:54
  245.4 6.6 %collective-permute-done.2 = bf16[48,3584]{1,0:T(8,128)(2,1)S(1)} collective-permute-done((bf16[48,3584]{1,0:T(8,128)(2,1)S(1)}, bf16[48,3584]{1,0:T(8,128)(2,1)S(1)}, u32[]{:S(2)}, u32[]{:S(2)}) %collective-permute-start.2) | collective-permute-done | bytes 344096 | tf_op jit(solution)/shard_map/ppermute | solution.py:54
  252.0 6.2 %collective-permute-done.9 = bf16[48,3584]{1,0:T(8,128)(2,1)S(1)} collective-permute-done((bf16[48,3584]{1,0:T(8,128)(2,1)S(1)}, bf16[48,3584]{1,0:T(8,128)(2,1)S(1)}, u32[]{:S(2)}, u32[]{:S(2)}) %collective-permute-start.9) | collective-permute-done | bytes 344096 | tf_op jit(solution)/shard_map/ppermute | solution.py:56
  258.1 5.8 %collective-permute-start.10 = (bf16[48,3584]{1,0:T(8,128)(2,1)S(1)}, bf16[48,3584]{1,0:T(8,128)(2,1)S(1)}, u32[]{:S(2)}, u32[]{:S(2)}) collective-permute-start(bf16[48,3584]{1,0:T(8,128)(2,1)S(1)} %collective-permute-done.9), channel_id=1, source_target_pairs={{8,0},{16,8},{24,16},{32,24},{40,32},{48,40},{56,48},{64,56},{72,6... | collective-permute-start | bytes 1032200 | tf_op jit(solution)/shard_map/ppermute | solution.py:56
  263.9 8.5 %collective-permute-done.3 = bf16[48,3584]{1,0:T(8,128)(2,1)S(1)} collective-permute-done((bf16[48,3584]{1,0:T(8,128)(2,1)S(1)}, bf16[48,3584]{1,0:T(8,128)(2,1)S(1)}, u32[]{:S(2)}, u32[]{:S(2)}) %collective-permute-start.3) | collective-permute-done | bytes 344096 | tf_op jit(solution)/shard_map/ppermute | solution.py:54
  283.3 6.7 %collective-permute-done.4 = bf16[48,3584]{1,0:T(8,128)(2,1)S(1)} collective-permute-done((bf16[48,3584]{1,0:T(8,128)(2,1)S(1)}, bf16[48,3584]{1,0:T(8,128)(2,1)S(1)}, u32[]{:S(2)}, u32[]{:S(2)}) %collective-permute-start.4) | collective-permute-done | bytes 344096 | tf_op jit(solution)/shard_map/ppermute | solution.py:54
  301.8 5.9 %collective-permute-start.13 = (bf16[48,3584]{1,0:T(8,128)(2,1)}, bf16[48,3584]{1,0:T(8,128)(2,1)}, u32[]{:S(2)}, u32[]{:S(2)}) collective-permute-start(bf16[48,3584]{1,0:T(8,128)(2,1)} %collective-permute-done.12), channel_id=1, source_target_pairs={{8,0},{16,8},{24,16},{32,24},{40,32},{48,40},{56,48},{64,56},{72,6... | collective-permute-start | bytes 1032200 | tf_op jit(solution)/shard_map/ppermute | solution.py:56
  343.7 6.0 %gather_fusion = bf16[16,48,3584]{2,1,0:T(8,128)(2,1)} fusion(bf16[16,48,3584]{2,1,0:T(8,128)(2,1)} %bitcast_dynamic-update-slice_fusion, s32[1024]{0:T(1024)S(1)} %pad_clamp_fusion), kind=kCustom, calls=%fused_computation | custom fusion | bytes 11010112 | tf_op jit(solution)/shard_map/gather | solution.py:59
  349.6 6.1 %fusion.10 = f32[768,512]{1,0:T(8,128)S(1)} fusion(bf16[768,3584]{1,0:T(8,128)(2,1)} %all-gather.3.cloned.1.call-done, bf16[512,3584]{1,0:T(8,128)(2,1)} %param.7), kind=kOutput, calls=%fused_computation.43 | convolution fusion | flops 2818572288 | bytes 10747904 | tf_op jit(solution)/shard_map/dot_general | solution.py:74
  355.7 15.9 %all-gather.5.cloned.1.call-done = bf16[768,3584]{1,0:T(8,128)(2,1)} async-done(((bf16[48,3584]{1,0:T(8,128)(2,1)}), bf16[768,3584]{1,0:T(8,128)(2,1)}) %all-gather.5.cloned.1.call-update) | async-done | bytes 5505040 | tf_op jit(solution)/shard_map/all_gather | solution.py:62
  371.6 7.6 %add_convert_fusion = bf16[768,512]{1,0:T(8,128)(2,1)} fusion(f32[768,512]{1,0:T(8,128)S(1)} %fusion.10, bf16[768,3584]{1,0:T(8,128)(2,1)} %all-gather.5.cloned.1.call-done, bf16[512,3584]{1,0:T(8,128)(2,1)} %param.8), kind=kOutput, calls=%fused_computation.13 | convolution fusion | flops 2819358720 | bytes 11534336 | tf_op jit(solution)/shard_map/dot_general | solution.py:77
  379.3 7.1 %multiply_convert_fusion = bf16[3584,512]{1,0:T(8,128)(2,1)} fusion(bf16[768,3584]{1,0:T(8,128)(2,1)} %bitcast.55, bf16[768,512]{1,0:T(8,128)(2,1)S(1)} %all_gather.13), kind=kOutput, calls=%fused_computation.7 | convolution fusion | flops 2822242304 | bytes 9961472 | tf_op jit(solution)/shard_map/dot_general | solution.py:65
  386.4 7.2 %fusion.4 = bf16[512,3584]{0,1:T(8,128)(2,1)} fusion(bf16[768,3584]{1,0:T(8,128)(2,1)} %all-gather.3.cloned.1.call-done, bf16[768,512]{1,0:T(8,128)(2,1)S(1)} %all_gather.12), kind=kOutput, calls=%fused_computation.11 | convolution fusion | flops 2822242304 | bytes 9961472 | tf_op jit(solution)/shard_map/dot_general | solution.py:68
  393.6 5.9 %copy.26 = bf16[512,3584]{1,0:T(8,128)(2,1)} copy(bf16[512,3584]{0,1:T(8,128)(2,1)} %fusion.4) | data formatting | bytes 7340032
  399.5 7.2 %fusion.5 = bf16[512,3584]{0,1:T(8,128)(2,1)} fusion(bf16[768,3584]{1,0:T(8,128)(2,1)} %all-gather.5.cloned.1.call-done, bf16[768,512]{1,0:T(8,128)(2,1)S(1)} %all_gather.12), kind=kOutput, calls=%fused_computation.12 | convolution fusion | flops 2822242304 | bytes 9961472 | tf_op jit(solution)/shard_map/dot_general | solution.py:71
  406.7 5.9 %copy.27 = bf16[512,3584]{1,0:T(8,128)(2,1)} copy(bf16[512,3584]{0,1:T(8,128)(2,1)} %fusion.5) | data formatting | bytes 7340032
  (68 shorter events, 73.2 us)
Async XLA Ops:
  7.2 201.4 %reduce-scatter.7.cloned.1.call-start = ((), (), s32[]{:S(2)}) async-start(), calls=%async_computation.5 | async-start | bytes 17547264 | tf_op jit(solution)/shard_map/reduce_scatter | solution.py:41
  97.8 251.8 %all-gather.3.cloned.1.call-start = ((), (), s32[]{:S(2)}) async-start(), calls=%async_computation.2 | async-start | bytes 5849088 | tf_op jit(solution)/shard_map/all_gather | solution.py:61
  211.1 160.5 %all-gather.5.cloned.1.call-start = ((), (), s32[]{:S(2)}) async-start(), calls=%async_computation.3 | async-start | bytes 5849088 | tf_op jit(solution)/shard_map/all_gather | solution.py:62
  211.2 12.8 %collective-permute-start = (bf16[48,3584]{1,0:T(8,128)(2,1)S(1)}, bf16[48,3584]{1,0:T(8,128)(2,1)S(1)}, u32[]{:S(2)}, u32[]{:S(2)}) collective-permute-start(bf16[48,3584]{1,0:T(8,128)(2,1)S(1)} %get-tuple-element.20), channel_id=1, source_target_pairs={{0,8},{8,16},{16,24},{24,32},{32,40},{40,48},{48,56},{56,64},{64,7... | collective-permute-start | bytes 1032200 | tf_op jit(solution)/shard_map/ppermute | solution.py:54
  224.0 16.0 %collective-permute-start.1 = (bf16[48,3584]{1,0:T(8,128)(2,1)S(1)}, bf16[48,3584]{1,0:T(8,128)(2,1)S(1)}, u32[]{:S(2)}, u32[]{:S(2)}) collective-permute-start(bf16[48,3584]{1,0:T(8,128)(2,1)S(1)} %collective-permute-done), channel_id=1, source_target_pairs={{0,8},{8,16},{16,24},{24,32},{32,40},{40,48},{48,56},{56,64},{64,7... | collective-permute-start | bytes 1032200 | tf_op jit(solution)/shard_map/ppermute | solution.py:54
  224.0 16.0 %collective-permute-start.8 = (bf16[48,3584]{1,0:T(8,128)(2,1)S(1)}, bf16[48,3584]{1,0:T(8,128)(2,1)S(1)}, u32[]{:S(2)}, u32[]{:S(2)}) collective-permute-start(bf16[48,3584]{1,0:T(8,128)(2,1)S(1)} %get-tuple-element.20), channel_id=1, source_target_pairs={{8,0},{16,8},{24,16},{32,24},{40,32},{48,40},{56,48},{64,56},{72,6... | collective-permute-start | bytes 1032200 | tf_op jit(solution)/shard_map/ppermute | solution.py:56
  240.0 12.0 %collective-permute-start.2 = (bf16[48,3584]{1,0:T(8,128)(2,1)S(1)}, bf16[48,3584]{1,0:T(8,128)(2,1)S(1)}, u32[]{:S(2)}, u32[]{:S(2)}) collective-permute-start(bf16[48,3584]{1,0:T(8,128)(2,1)S(1)} %collective-permute-done.1), channel_id=1, source_target_pairs={{0,8},{8,16},{16,24},{24,32},{32,40},{40,48},{48,56},{56,64},{64,7... | collective-permute-start | bytes 1032200 | tf_op jit(solution)/shard_map/ppermute | solution.py:54
  240.0 18.1 %collective-permute-start.9 = (bf16[48,3584]{1,0:T(8,128)(2,1)S(1)}, bf16[48,3584]{1,0:T(8,128)(2,1)S(1)}, u32[]{:S(2)}, u32[]{:S(2)}) collective-permute-start(bf16[48,3584]{1,0:T(8,128)(2,1)S(1)} %collective-permute-done.8), channel_id=1, source_target_pairs={{8,0},{16,8},{24,16},{32,24},{40,32},{48,40},{56,48},{64,56},{72,6... | collective-permute-start | bytes 1032200 | tf_op jit(solution)/shard_map/ppermute | solution.py:56
  252.0 25.5 %copy-start = (bf16[48,3584]{1,0:T(8,128)(2,1)}, bf16[48,3584]{1,0:T(8,128)(2,1)S(1)}, u32[]{:S(2)}) copy-start(bf16[48,3584]{1,0:T(8,128)(2,1)S(1)} %collective-permute-done.2) | copy-start | bytes 1032196
  252.0 20.5 %collective-permute-start.3 = (bf16[48,3584]{1,0:T(8,128)(2,1)S(1)}, bf16[48,3584]{1,0:T(8,128)(2,1)S(1)}, u32[]{:S(2)}, u32[]{:S(2)}) collective-permute-start(bf16[48,3584]{1,0:T(8,128)(2,1)S(1)} %collective-permute-done.2), channel_id=1, source_target_pairs={{0,8},{8,16},{16,24},{24,32},{32,40},{40,48},{48,56},{56,64},{64,7... | collective-permute-start | bytes 1032200 | tf_op jit(solution)/shard_map/ppermute | solution.py:54
  258.1 19.3 %collective-permute-start.10 = (bf16[48,3584]{1,0:T(8,128)(2,1)S(1)}, bf16[48,3584]{1,0:T(8,128)(2,1)S(1)}, u32[]{:S(2)}, u32[]{:S(2)}) collective-permute-start(bf16[48,3584]{1,0:T(8,128)(2,1)S(1)} %collective-permute-done.9), channel_id=1, source_target_pairs={{8,0},{16,8},{24,16},{32,24},{40,32},{48,40},{56,48},{64,56},{72,6... | collective-permute-start | bytes 1032200 | tf_op jit(solution)/shard_map/ppermute | solution.py:56
  272.4 29.4 %copy-start.5 = (bf16[48,3584]{1,0:T(8,128)(2,1)}, bf16[48,3584]{1,0:T(8,128)(2,1)S(1)}, u32[]{:S(2)}) copy-start(bf16[48,3584]{1,0:T(8,128)(2,1)S(1)} %collective-permute-done.3) | copy-start | bytes 1032196
  272.4 17.6 %collective-permute-start.4 = (bf16[48,3584]{1,0:T(8,128)(2,1)S(1)}, bf16[48,3584]{1,0:T(8,128)(2,1)S(1)}, u32[]{:S(2)}, u32[]{:S(2)}) collective-permute-start(bf16[48,3584]{1,0:T(8,128)(2,1)S(1)} %collective-permute-done.3), channel_id=1, source_target_pairs={{0,8},{8,16},{16,24},{24,32},{32,40},{40,48},{48,56},{56,64},{64,7... | collective-permute-start | bytes 1032200 | tf_op jit(solution)/shard_map/ppermute | solution.py:54
  277.5 12.5 %collective-permute-start.11 = (bf16[48,3584]{1,0:T(8,128)(2,1)S(1)}, bf16[48,3584]{1,0:T(8,128)(2,1)S(1)}, u32[]{:S(2)}, u32[]{:S(2)}) collective-permute-start(bf16[48,3584]{1,0:T(8,128)(2,1)S(1)} %collective-permute-done.10), channel_id=1, source_target_pairs={{8,0},{16,8},{24,16},{32,24},{40,32},{48,40},{56,48},{64,56},{72,6... | collective-permute-start | bytes 1032200 | tf_op jit(solution)/shard_map/ppermute | solution.py:56
  290.0 17.7 %copy-start.6 = (bf16[48,3584]{1,0:T(8,128)(2,1)}, bf16[48,3584]{1,0:T(8,128)(2,1)S(1)}, u32[]{:S(2)}) copy-start(bf16[48,3584]{1,0:T(8,128)(2,1)S(1)} %collective-permute-done.4) | copy-start | bytes 1032196
  290.0 11.8 %collective-permute-start.5 = (bf16[48,3584]{1,0:T(8,128)(2,1)S(1)}, bf16[48,3584]{1,0:T(8,128)(2,1)S(1)}, u32[]{:S(2)}, u32[]{:S(2)}) collective-permute-start(bf16[48,3584]{1,0:T(8,128)(2,1)S(1)} %collective-permute-done.4), channel_id=1, source_target_pairs={{0,8},{8,16},{16,24},{24,32},{32,40},{40,48},{48,56},{56,64},{64,7... | collective-permute-start | bytes 1032200 | tf_op jit(solution)/shard_map/ppermute | solution.py:54
  290.8 11.0 %collective-permute-start.12 = (bf16[48,3584]{1,0:T(8,128)(2,1)S(1)}, bf16[48,3584]{1,0:T(8,128)(2,1)}, u32[]{:S(2)}, u32[]{:S(2)}) collective-permute-start(bf16[48,3584]{1,0:T(8,128)(2,1)S(1)} %collective-permute-done.11), channel_id=1, source_target_pairs={{8,0},{16,8},{24,16},{32,24},{40,32},{48,40},{56,48},{64,56},{72,6... | collective-permute-start | bytes 1032200 | tf_op jit(solution)/shard_map/ppermute | solution.py:56
  301.8 10.9 %collective-permute-start.6 = (bf16[48,3584]{1,0:T(8,128)(2,1)S(1)}, bf16[48,3584]{1,0:T(8,128)(2,1)}, u32[]{:S(2)}, u32[]{:S(2)}) collective-permute-start(bf16[48,3584]{1,0:T(8,128)(2,1)S(1)} %collective-permute-done.5), channel_id=1, source_target_pairs={{0,8},{8,16},{16,24},{24,32},{32,40},{40,48},{48,56},{56,64},{64,7... | collective-permute-start | bytes 1032200 | tf_op jit(solution)/shard_map/ppermute | solution.py:54
  301.8 11.0 %collective-permute-start.13 = (bf16[48,3584]{1,0:T(8,128)(2,1)}, bf16[48,3584]{1,0:T(8,128)(2,1)}, u32[]{:S(2)}, u32[]{:S(2)}) collective-permute-start(bf16[48,3584]{1,0:T(8,128)(2,1)} %collective-permute-done.12), channel_id=1, source_target_pairs={{8,0},{16,8},{24,16},{32,24},{40,32},{48,40},{56,48},{64,56},{72,6... | collective-permute-start | bytes 1032200 | tf_op jit(solution)/shard_map/ppermute | solution.py:56
  312.7 10.9 %collective-permute-start.7 = (bf16[48,3584]{1,0:T(8,128)(2,1)}, bf16[48,3584]{1,0:T(8,128)(2,1)}, u32[]{:S(2)}, u32[]{:S(2)}) collective-permute-start(bf16[48,3584]{1,0:T(8,128)(2,1)} %collective-permute-done.6), channel_id=1, source_target_pairs={{0,8},{8,16},{16,24},{24,32},{32,40},{40,48},{48,56},{56,64},{64,7... | collective-permute-start | bytes 1032200 | tf_op jit(solution)/shard_map/ppermute | solution.py:54
  312.8 99.9 %reduce-scatter.5.cloned.1.call-start = ((), (), s32[]{:S(2)}) async-start(), calls=%async_computation.4 | async-start | bytes 884736 | tf_op jit(solution)/shard_map/reduce_scatter | solution.py:84
  312.8 25.1 %copy-start.2 = (bf16[48,3584]{1,0:T(8,128)(2,1)S(1)}, bf16[48,3584]{1,0:T(8,128)(2,1)}, u32[]{:S(2)}) copy-start(bf16[48,3584]{1,0:T(8,128)(2,1)} %copy-done.1) | copy-start | bytes 1032196
  312.8 25.8 %copy-start.4 = (bf16[48,3584]{1,0:T(8,128)(2,1)S(1)}, bf16[48,3584]{1,0:T(8,128)(2,1)}, u32[]{:S(2)}) copy-start(bf16[48,3584]{1,0:T(8,128)(2,1)} %copy-done.3) | copy-start | bytes 1032196
  312.9 30.1 %collective-permute-start.14 = (bf16[48,3584]{1,0:T(8,128)(2,1)}, bf16[48,3584]{1,0:T(8,128)(2,1)S(1)}, u32[]{:S(2)}, u32[]{:S(2)}) collective-permute-start(bf16[48,3584]{1,0:T(8,128)(2,1)} %collective-permute-done.13), channel_id=1, source_target_pairs={{8,0},{16,8},{24,16},{32,24},{40,32},{48,40},{56,48},{64,56},{72,6... | collective-permute-start | bytes 1032200 | tf_op jit(solution)/shard_map/ppermute | solution.py:56
  (3 other events, 17.5 us)
Sparse Core Ops, SparseCore 0:
  97.9 110.5 reduce-scatter.6
  211.5 77.0 all-gather.2
  312.9 58.7 all-gather.4
  379.4 31.2 reduce-scatter.4
